TPU v7x, 32 devices: a whole 2x2x4 slice. The times are simulated.
32 devices in a mesh: group: 2 (over x), seq: 16 (over z, y, core).
Axes of the slice: x: 2, y: 2, z: 4, core: 2. Of those that a mesh axis runs over, the one named last changes fastest.
Arguments:
- queries: bfloat16 [8192, 768], P(('group', 'seq')), parts along dimension 0, may hold values from -6 to 6
- key_rows: bfloat16 [8192, 768], P(('group', 'seq')), parts along dimension 0, may hold values from -6 to 6
- value_rows: bfloat16 [8192, 768], P(('group', 'seq')), parts along dimension 0, may hold values from -20 to 20
- dilation: int32 [12], replicated, may hold values from 2 to 30, as said below
- global_rows: int32 [128], P('group'), parts along dimension 0, may hold values from 0 to 4095, as said below
- out_weight: bfloat16 [768, 1536], replicated, may hold values from -0.21875 to 0.21875
- mlp_up: bfloat16 [1536, 3072], P('seq'), may hold values from -0.15625 to 0.15625
- mlp_down: bfloat16 [3072, 1536], P('seq'), may hold values from -0.109375 to 0.109375
Outputs:
- attended: bfloat16 [8192, 1536], P(('group', 'seq')), parts along dimension 0
- mlp_out: bfloat16 [8192, 1536], P(('group', 'seq')), parts along dimension 0
There are 2 independent parts, one for each index of `group`. A program takes and returns all parts, laid end to end along the dimension named above; an argument that names none is the same for every part. Nothing has to cross between parts.
Inputs may be any that keep to these rules, and one draw needn't show every extreme that they name: `dilation`: each offset is a multiple of 2; some head has the smallest and some the largest. `global_rows`: distinct positions.
All inputs are finite; a program needn't handle non-finite values.
Results may differ from a plain program's by a relative error of at most 0.0071.
Values may be sent and summed in bfloat16 or wider, within the bound.
A program may use at most 192 MiB of HBM per device.

v0:
```python
import jax
import jax.numpy as jnp
from jax import lax
from jax.sharding import PartitionSpec as P

H = 12
DH = 64
BLK = 128
GLOBALS = 64


def with_halo(cells, sides, width):
    for axis, dim in sides:
        count = lax.axis_size(axis)
        head = lax.slice_in_dim(cells, 0, width, axis=dim)
        tail = lax.slice_in_dim(cells, cells.shape[dim] - width, cells.shape[dim], axis=dim)
        cells = jnp.concatenate(
            [
                lax.ppermute(tail, axis, [(i, (i + 1) % count) for i in range(count)]),
                cells,
                lax.ppermute(head, axis, [((i + 1) % count, i) for i in range(count)]),
            ],
            axis=dim,
        )
    return cells


def passed_along(value, axis, steps):
    count = lax.axis_size(axis)
    pairs = [(source, (source + steps) % count) for source in range(count)]
    return lax.ppermute(value, axis, pairs)


def merged_2(part, axis, combine):
    gathered = jax.tree.map(lambda a: lax.all_gather(a, axis), part)

    def take(source):
        return jax.tree.map(lambda a: lax.dynamic_index_in_dim(a, source, 0, False), gathered)

    return lax.fori_loop(
        1, lax.axis_size(axis), lambda source, state: combine(state, take(source)), take(0)
    )


def attend_blocks(query_blocks, local_keys, local_values, glob_keys, glob_values):
    count = query_blocks.shape[0]
    keys_all = jnp.concatenate(
        [local_keys, jnp.broadcast_to(glob_keys[None], (count,) + glob_keys.shape)], axis=1
    )
    values_all = jnp.concatenate(
        [local_values, jnp.broadcast_to(glob_values[None], (count,) + glob_values.shape)], axis=1
    )
    scores = jnp.einsum(
        "nqhd,nkhd->nhqk", query_blocks, keys_all, preferred_element_type=jnp.float32
    ) * DH ** (-0.5)
    peak = jnp.max(scores, axis=-1, keepdims=True)
    exp_terms = jnp.exp(scores - peak)
    totals = jnp.sum(exp_terms, axis=-1, keepdims=True)
    weights = (exp_terms / totals).astype(jnp.bfloat16)
    return jnp.einsum("nhqk,nkhd->nqhd", weights, values_all, preferred_element_type=jnp.float32)


def select_heads(chosen, arrived, current):
    shaped = current.shape
    head_mask = chosen[None, None, :, None]
    merged = jnp.where(
        head_mask,
        arrived.reshape(shaped[0], shaped[1], H, DH),
        current.reshape(shaped[0], shaped[1], H, DH),
    )
    return merged.reshape(shaped)


def join_partials(first, second):
    peak_first, total_first, numer_first = first
    peak_second, total_second, numer_second = second
    highest = jnp.maximum(peak_first, peak_second)
    scale_first = jnp.exp(peak_first - highest)
    scale_second = jnp.exp(peak_second - highest)
    return (
        highest,
        total_first * scale_first + total_second * scale_second,
        numer_first * scale_first[:, :, None] + numer_second * scale_second[:, :, None],
    )


def per_device(queries, key_rows, value_rows, dilation, global_rows, out_weight, mlp_up, mlp_down):
    tok_rows = queries.shape[0]
    blocks = tok_rows // BLK
    devices = lax.axis_size("seq")
    stacked = jnp.stack([key_rows, value_rows])
    padded = with_halo(stacked, (("seq", 1),), BLK)
    dev_hops = dilation // blocks
    current = stacked
    for bit_level in range((devices - 1).bit_length()):
        arrived = passed_along(current, "seq", -(1 << bit_level))
        chosen = dev_hops >> bit_level & 1 == 1
        current = select_heads(chosen, arrived, current)
    start = lax.axis_index("seq") * tok_rows
    offsets = global_rows - start
    onehot = offsets[:, None] == jnp.arange(tok_rows, dtype=jnp.int32)[None, :]
    picker = onehot.astype(jnp.bfloat16)
    picked = (
        jnp.dot(picker, queries, preferred_element_type=jnp.float32),
        jnp.dot(picker, key_rows, preferred_element_type=jnp.float32),
        jnp.dot(picker, value_rows, preferred_element_type=jnp.float32),
    )
    glob_q, glob_k, glob_v = lax.psum((picked[0], picked[1], picked[2]), "seq")
    glob_query = glob_q.astype(jnp.bfloat16).reshape(GLOBALS, H, DH)
    glob_keys = glob_k.astype(jnp.bfloat16).reshape(GLOBALS, H, DH)
    glob_values = glob_v.astype(jnp.bfloat16).reshape(GLOBALS, H, DH)
    grid = padded.reshape(2, blocks + 2, BLK, H, DH)
    dilated = current.reshape(2, blocks, BLK, H, DH)
    local_set = jnp.concatenate([grid[:, :-2], grid[:, 1:-1], grid[:, 2:], dilated], axis=2)
    attended_local = attend_blocks(
        queries.reshape(blocks, BLK, H, DH), local_set[0], local_set[1], glob_keys, glob_values
    ).reshape(tok_rows, H * DH)
    scores = jnp.einsum(
        "ghd,thd->hgt",
        glob_query,
        key_rows.reshape(tok_rows, H, DH),
        preferred_element_type=jnp.float32,
    ) * DH ** (-0.5)
    peak = jnp.max(scores, axis=2)
    exp_terms = jnp.exp(scores - peak[:, :, None])
    totals = jnp.sum(exp_terms, axis=2)
    numerators = jnp.einsum(
        "hgt,thd->hgd",
        exp_terms,
        value_rows.astype(jnp.float32).reshape(tok_rows, H, DH),
        precision=lax.Precision.HIGHEST,
    )
    peak, totals, numerators = merged_2((peak, totals, numerators), "seq", join_partials)
    glob_out = (numerators / totals[:, :, None]).transpose(1, 0, 2).reshape(GLOBALS, H * DH)
    onehot_float = onehot.astype(jnp.float32)
    placed = jnp.dot(onehot_float.T, glob_out, precision=lax.Precision.HIGHEST)
    owned_rows = jnp.sum(onehot_float, axis=0) > 0.5
    attention = jnp.where(owned_rows[:, None], placed, attended_local).astype(jnp.bfloat16)
    attended = jnp.dot(attention, out_weight, preferred_element_type=jnp.float32).astype(
        jnp.bfloat16
    )
    columns = attended
    pre_act = jnp.dot(
        columns,
        lax.all_gather(mlp_up, "seq", axis=0, tiled=True),
        preferred_element_type=jnp.float32,
    )
    hidden = jax.nn.gelu(pre_act, approximate=True).astype(jnp.bfloat16)
    columns = hidden
    mlp_out = jnp.dot(
        columns,
        lax.all_gather(mlp_down, "seq", axis=0, tiled=True),
        preferred_element_type=jnp.float32,
    ).astype(jnp.bfloat16)
    return (attended, mlp_out)


def solution(mesh):
    placed = (
        P(("group", "seq"), None),
        P(("group", "seq"), None),
        P(("group", "seq"), None),
        P(),
        P("group"),
        P(),
        P("seq", None),
        P("seq", None),
    )
    return jax.shard_map(
        per_device,
        mesh=mesh,
        in_specs=placed,
        out_specs=(P(("group", "seq"), None), P(("group", "seq"), None)),
        check_vma=False,
    )
```

profile of v0, /device:TPU:0, one launch (start us, length us, event | category | flops | bytes accessed | tf_op | source)
XLA Modules:
  0.0 397.6 jit_solution(10071234965016458596)
XLA Ops:
  9.2 1.9 fusion.47
  11.1 1.9 fusion.48
  13.0 2.0 copy.69
  15.0 2.0 fusion.49
  17.0 70.1 %all-reduce.2 = (bf16[64,768]{1,0:T(8,128)(2,1)}, bf16[64,768]{1,0:T(8,128)(2,1)}, bf16[64,768]{1,0:T(8,128)(2,1)}) all-reduce(f32[64,768]{1,0:T(8,128)} %fusion.47, f32[64,768]{1,0:T(8,128)} %fusion.48, f32[64,768]{1,0:T(8,128)} %fusion.49), channel_id=1, replica_groups=mesh['group'=2,'seq'=16] {'seq'}, use_global_device_ids=true, to_apply=%region_7.8 | all-reduce | flops 147456 | bytes 884736 | tf_op jit(solution)/shard_map/psum | solution.py:108
  87.1 1.8 reshape.87
  91.1 2.4 fusion.37
  97.8 19.8 %collective-permute-done.2 = bf16[2,256,768]{2,1,0:T(8,128)(2,1)} collective-permute-done((bf16[2,256,768]{2,1,0:T(8,128)(2,1)}, bf16[2,256,768]{2,1,0:T(8,128)(2,1)}, u32[]{:S(2)}, u32[]{:S(2)}) %collective-permute-start.2) | collective-permute-done | bytes 786464 | tf_op jit(solution)/shard_map/ppermute | solution.py:31
  117.6 2.1 broadcast_select_fusion
  121.1 17.6 %collective-permute-done.3 = bf16[2,256,768]{2,1,0:T(8,128)(2,1)} collective-permute-done((bf16[2,256,768]{2,1,0:T(8,128)(2,1)}, bf16[2,256,768]{2,1,0:T(8,128)(2,1)}, u32[]{:S(2)}, u32[]{:S(2)}) %collective-permute-start.3) | collective-permute-done | bytes 786464 | tf_op jit(solution)/shard_map/ppermute | solution.py:31
  138.8 2.4 broadcast_select_fusion.1
  142.1 15.3 %collective-permute-start = (bf16[2,128,768]{2,1,0:T(8,128)(2,1)}, bf16[2,128,768]{2,1,0:T(8,128)(2,1)}, u32[]{:S(2)}, u32[]{:S(2)}) collective-permute-start(bf16[2,128,768]{2,1,0:T(8,128)(2,1)} %get-tuple-element.209), channel_id=1, source_target_pairs={{0,1},{1,2},{2,3},{3,4},{4,5},{5,6},{6,7},{7,8},{8,9},{9,10},{10,1... | collective-permute-start | bytes 1179656 | tf_op jit(solution)/shard_map/ppermute | solution.py:19
  157.4 4.5 %collective-permute-start.1 = (bf16[2,128,768]{2,1,0:T(8,128)(2,1)}, bf16[2,128,768]{2,1,0:T(8,128)(2,1)}, u32[]{:S(2)}, u32[]{:S(2)}) collective-permute-start(bf16[2,128,768]{2,1,0:T(8,128)(2,1)} %get-tuple-element.210), channel_id=1, source_target_pairs={{1,0},{2,1},{3,2},{4,3},{5,4},{6,5},{7,6},{8,7},{9,8},{10,9},{11,1... | collective-permute-start | bytes 1179656 | tf_op jit(solution)/shard_map/ppermute | solution.py:21
  162.7 1.9 stack.19
  164.6 2.0 copy.89
  168.4 1.8 copy.82
  170.2 1.7 copy.94
  171.9 1.8 reshape.96
  173.8 1.7 copy.93
  175.5 1.5 fusion.38
  176.9 23.6 %all-gather.4 = f32[16,12,64]{2,1,0:T(8,128)S(1)} all-gather(f32[1,12,64]{2,1,0:T(8,128)S(1)} %bitcast.103), channel_id=3, replica_groups=mesh['group'=2,'seq'=16] {'seq'}, dimensions={0}, use_global_device_ids=true | all-gather | bytes 52224 | tf_op jit(solution)/shard_map/all_gather | solution.py:35
  200.6 18.3 %all-gather.3 = f32[16,12,64]{2,1,0:T(8,128)S(1)} all-gather(f32[1,12,64]{2,1,0:T(8,128)S(1)} %bitcast.102), channel_id=2, replica_groups=mesh['group'=2,'seq'=16] {'seq'}, dimensions={0}, use_global_device_ids=true | all-gather | bytes 52224 | tf_op jit(solution)/shard_map/all_gather | solution.py:35
  219.5 2.4 broadcast_select_fusion.2
  222.5 2.4 pad_maximum_fusion.2
  224.9 2.6 copy.71
  227.5 3.5 reshape.91
  231.0 5.1 %fusion.65 = (bf16[2,2,128,12,64]{2,1,4,3,0:T(2,128)(2,1)S(1)}, bf16[2,2,128,12,64]{2,1,4,3,0:T(2,128)(2,1)S(1)}, bf16[2,2,128,12,64]{2,1,4,3,0:T(2,128)(2,1)S(1)}) fusion(bf16[2,4,128,12,64]{2,1,4,3,0:T(4,128)(2,1)} %reshape.91), kind=kLoop, calls=%fused_computation.98 | loop fusion | bytes 4718592 | tf_op jit(solution)/shard_map/slice | solution.py:114
  238.6 2.3 copy.78
  240.9 2.8 reshape.95
  243.7 2.3 copy.77
  246.0 2.7 reshape.94
  248.7 2.3 copy.76
  251.0 2.7 reshape.93
  253.7 39.6 %collective-permute-done.5 = bf16[2,256,768]{2,1,0:T(8,128)(2,1)} collective-permute-done((bf16[2,256,768]{2,1,0:T(8,128)(2,1)}, bf16[2,256,768]{2,1,0:T(8,128)(2,1)}, u32[]{:S(2)}, u32[]{:S(2)}) %collective-permute-start.5) | collective-permute-done | bytes 786464 | tf_op jit(solution)/shard_map/ppermute | solution.py:31
  293.3 2.3 copy.75
  295.6 2.7 reshape.92
  298.3 2.6 fusion.36
  301.6 1.9 slice_bitcast_fusion.1
  303.6 7.2 %fusion.66 = (f32[2,12,128]{2,1,0:T(8,128)S(1)}, f32[2,12,128,576]{2,3,1,0:T(8,128)}) fusion(bf16[2,64,12,64]{1,3,2,0:T(8,128)(2,1)S(1)} %broadcast_in_dim.97, bf16[2,512,12,64]{1,3,2,0:T(8,128)(2,1)} %get-tuple-element.205, bf16[2,128,12,64]{1,0,3,2:T(2,128)(2,1)S(1)} %copy-done.8), kind=kOutput, calls=%fused_computation.99 | convolution fusion | flops 235340352 | bytes 9252864 | tf_op jit(solution)/shard_map/sub | solution.py:57
  310.9 4.3 %fusion.30 = bf16[2,128,12,64]{1,3,2,0:T(8,128)(2,1)S(1)} fusion(f32[2,12,128,576]{2,3,1,0:T(8,128)} %get-tuple-element.215, f32[2,12,128]{2,1,0:T(8,128)S(1)} %get-tuple-element.214, bf16[2,64,12,64]{1,3,2,0:T(8,128)(2,1)S(1)} %broadcast_in_dim.95, bf16[2,512,12,64]{1,3,2,0:T(8,128)(2,1)} %get-tuple-element.204), kind=kOutput, calls=%fused_computation.42 | convolution fusion | flops 233570304 | bytes 9252864 | tf_op jit(solution)/shard_map/nhqk,nkhd->nqhd/dot_general | solution.py:60
  317.0 32.2 %while.19 = (s32[]{:T(128)}, f32[12,64]{1,0:T(8,128)S(1)}, f32[12,64]{1,0:T(8,128)S(1)}, f32[12,64,64]{2,1,0:T(8,128)S(1)}, f32[16,12,64]{2,1,0:T(8,128)}, /*ind...) while((s32[]{:T(128)}, f32[12,64]{1,0:T(8,128)S(1)}, ...), condition=%wide.region_5.6_spmd, body=%wide.region_4.5_spmd.sunk | while | flops 152069 | bytes 620695 | solution.py:40
  319.8 1.4 fusion.88
  328.4 1.4 fusion.88
  332.7 1.5 fusion.88
  339.2 1.4 fusion.88
  343.5 1.4 fusion.88
  351.2 27.4 %all-gather.9.cloned.1.call-done = bf16[1536,3072]{1,0:T(8,128)(2,1)} async-done(((bf16[96,3072]{1,0:T(8,128)(2,1)}), bf16[1536,3072]{1,0:T(8,128)(2,1)}) %all-gather.9.cloned.1.call-update) | async-done | bytes 9437200 | tf_op jit(solution)/shard_map/all_gather | solution.py:145
  378.6 12.4 %convolution_convert_fusion = bf16[256,1536]{1,0:T(8,128)(2,1)} fusion(bf16[3072,1536]{1,0:T(8,128)(2,1)} %all-gather.11.cloned.1.call-done, bf16[256,1536]{1,0:T(8,128)(2,1)S(1)} %convolution_convert_fusion.1, bf16[1536,3072]{1,0:T(8,128)(2,1)} %all-gather.9.cloned.1.call-done), kind=kOutput, calls=%fused_computation.28 | convolution fusion | flops 4839309312 | bytes 20447232 | tf_op jit(solution)/shard_map/dot_general | solution.py:150
  (112 shorter events, 46.5 us)
Async XLA Ops:
  7.2 343.2 %copy-start = (bf16[768,1536]{1,0:T(8,128)(2,1)S(1)}, bf16[768,1536]{1,0:T(8,128)(2,1)}, u32[]{:S(2)}) copy-start(bf16[768,1536]{1,0:T(8,128)(2,1)} %param.15) | copy-start | bytes 7077892
  7.2 308.7 %all-gather.13.cloned.1.call-start = ((), (), s32[]{:S(2)}) async-start(), calls=%async_computation.2 | async-start | bytes 6684672 | tf_op jit(solution)/shard_map/all_gather | solution.py:35
  9.2 79.7 %copy-start.11 = (s32[64]{0:T(128)}, s32[64]{0:T(128)S(1)}, u32[]{:S(2)}) copy-start(s32[64]{0:T(128)S(1)} %broadcast_subtract_fusion) | copy-start | bytes 772
  15.0 80.0 %copy-start.1 = (bf16[256,768]{1,0:T(8,128)(2,1)S(1)}, bf16[256,768]{1,0:T(8,128)(2,1)}, u32[]{:S(2)}) copy-start(bf16[256,768]{1,0:T(8,128)(2,1)} %param.11) | copy-start | bytes 1179652
  15.0 80.0 %copy-start.2 = (bf16[256,768]{1,0:T(8,128)(2,1)S(1)}, bf16[256,768]{1,0:T(8,128)(2,1)}, u32[]{:S(2)}) copy-start(bf16[256,768]{1,0:T(8,128)(2,1)} %param.12) | copy-start | bytes 1179652
  88.9 7.0 %copy-start.17 = (s32[12]{0:T(128)S(1)}, s32[12]{0:T(128)}, u32[]{:S(2)}) copy-start(s32[12]{0:T(128)} %param.13) | copy-start | bytes 148
  90.2 0.9 copy-start.3
  93.5 257.7 %all-gather.11.cloned.1.call-start = ((), (), s32[]{:S(2)}) async-start(), calls=%async_computation.1 | async-start | bytes 10027008 | tf_op jit(solution)/shard_map/all_gather | solution.py:152
  94.2 284.4 %all-gather.9.cloned.1.call-start = ((), (), s32[]{:S(2)}) async-start(), calls=%async_computation | async-start | bytes 10027008 | tf_op jit(solution)/shard_map/all_gather | solution.py:145
  95.9 21.7 %collective-permute-start.2 = (bf16[2,256,768]{2,1,0:T(8,128)(2,1)}, bf16[2,256,768]{2,1,0:T(8,128)(2,1)}, u32[]{:S(2)}, u32[]{:S(2)}) collective-permute-start(bf16[2,256,768]{2,1,0:T(8,128)(2,1)} %pad_maximum_fusion.9), channel_id=1, source_target_pairs={{0,15},{1,0},{2,1},{3,2},{4,3},{5,4},{6,5},{7,6},{8,7},{9,8},{10,9... | collective-permute-start | bytes 2359304 | tf_op jit(solution)/shard_map/ppermute | solution.py:31
  97.1 0.6 copy-start.15
  119.8 19.0 %collective-permute-start.3 = (bf16[2,256,768]{2,1,0:T(8,128)(2,1)}, bf16[2,256,768]{2,1,0:T(8,128)(2,1)}, u32[]{:S(2)}, u32[]{:S(2)}) collective-permute-start(bf16[2,256,768]{2,1,0:T(8,128)(2,1)} %broadcast_select_fusion), channel_id=1, source_target_pairs={{0,14},{1,15},{2,0},{3,1},{4,2},{5,3},{6,4},{7,5},{8,6},{9,7},{10,... | collective-permute-start | bytes 2359304 | tf_op jit(solution)/shard_map/ppermute | solution.py:31
  121.1 45.5 %copy-start.14 = (pred[12]{0:T(512)(128)(4,1)S(1)}, pred[12]{0:T(512)(128)(4,1)}, u32[]{:S(2)}) copy-start(pred[12]{0:T(512)(128)(4,1)} %get-tuple-element.211) | copy-start | bytes 40
  141.1 78.4 %collective-permute-start.4 = (bf16[2,256,768]{2,1,0:T(8,128)(2,1)}, bf16[2,256,768]{2,1,0:T(8,128)(2,1)}, u32[]{:S(2)}, u32[]{:S(2)}) collective-permute-start(bf16[2,256,768]{2,1,0:T(8,128)(2,1)} %broadcast_select_fusion.1), channel_id=1, source_target_pairs={{0,12},{1,13},{2,14},{3,15},{4,0},{5,1},{6,2},{7,3},{8,4},{9,5},{1... | collective-permute-start | bytes 2359304 | tf_op jit(solution)/shard_map/ppermute | solution.py:31
  142.1 80.4 %collective-permute-start = (bf16[2,128,768]{2,1,0:T(8,128)(2,1)}, bf16[2,128,768]{2,1,0:T(8,128)(2,1)}, u32[]{:S(2)}, u32[]{:S(2)}) collective-permute-start(bf16[2,128,768]{2,1,0:T(8,128)(2,1)} %get-tuple-element.209), channel_id=1, source_target_pairs={{0,1},{1,2},{2,3},{3,4},{4,5},{5,6},{6,7},{7,8},{8,9},{9,10},{10,1... | collective-permute-start | bytes 1179656 | tf_op jit(solution)/shard_map/ppermute | solution.py:19
  157.4 61.5 %copy-start.12 = (s32[64]{0:T(128)S(1)}, s32[64]{0:T(128)}, u32[]{:S(2)}) copy-start(s32[64]{0:T(128)} %copy-done.11) | copy-start | bytes 772
  157.4 65.1 %collective-permute-start.1 = (bf16[2,128,768]{2,1,0:T(8,128)(2,1)}, bf16[2,128,768]{2,1,0:T(8,128)(2,1)}, u32[]{:S(2)}, u32[]{:S(2)}) collective-permute-start(bf16[2,128,768]{2,1,0:T(8,128)(2,1)} %get-tuple-element.210), channel_id=1, source_target_pairs={{1,0},{2,1},{3,2},{4,3},{5,4},{6,5},{7,6},{8,7},{9,8},{10,9},{11,1... | collective-permute-start | bytes 1179656 | tf_op jit(solution)/shard_map/ppermute | solution.py:21
  200.6 18.4 %copy-start.9 = (f32[16,12,64]{2,1,0:T(8,128)}, f32[16,12,64]{2,1,0:T(8,128)S(1)}, u32[]{:S(2)}) copy-start(f32[16,12,64]{2,1,0:T(8,128)S(1)} %all-gather.4) | copy-start | bytes 147460
  218.8 0.7 copy-start.10
  221.9 71.4 %collective-permute-start.5 = (bf16[2,256,768]{2,1,0:T(8,128)(2,1)}, bf16[2,256,768]{2,1,0:T(8,128)(2,1)}, u32[]{:S(2)}, u32[]{:S(2)}) collective-permute-start(bf16[2,256,768]{2,1,0:T(8,128)(2,1)} %broadcast_select_fusion.2), channel_id=1, source_target_pairs={{0,8},{1,9},{2,10},{3,11},{4,12},{5,13},{6,14},{7,15},{8,0},{9,1},... | collective-permute-start | bytes 2359304 | tf_op jit(solution)/shard_map/ppermute | solution.py:31
  298.3 2.6 copy-start.4
  298.3 2.6 copy-start.5
  301.6 1.9 copy-start.7
  301.6 2.0 copy-start.8
  303.6 7.2 %copy-start.6 = (bf16[64,768]{0,1:T(8,128)(2,1)S(1)}, bf16[64,768]{0,1:T(8,128)(2,1)}, u32[]{:S(2)}) copy-start(bf16[64,768]{0,1:T(8,128)(2,1)} %copy.93) | copy-start | bytes 294916
  316.9 32.8 %copy-start.13 = (s32[64]{0:T(128)S(1)}, s32[64]{0:T(128)}, u32[]{:S(2)}) copy-start(s32[64]{0:T(128)} %copy-done.11) | copy-start | bytes 772
  316.9 32.8 %copy-start.16 = (pred[256]{0:T(512)(128)(4,1)S(1)}, pred[256]{0:T(512)(128)(4,1)}, u32[]{:S(2)}) copy-start(pred[256]{0:T(512)(128)(4,1)} %broadcast_compare_fusion) | copy-start | bytes 772
  351.1 39.9 %copy-start.18 = (bf16[256,1536]{1,0:T(8,128)(2,1)}, bf16[256,1536]{1,0:T(8,128)(2,1)S(1)}, u32[]{:S(2)}) copy-start(bf16[256,1536]{1,0:T(8,128)(2,1)S(1)} %convolution_convert_fusion.1) | copy-start | bytes 2359300
Sparse Core Ops, SparseCore 0:
  93.6 83.7 all-gather.12
  179.7 116.0 all-gather.10
  298.1 80.4 all-gather.8
where the time goes:
time: 400 us; the launch traced here: 398 us
  blocking collectives  112 us (28%)
  waiting for transfers between devices  106 us (26%)
  local copies, waits for them, and re-layouts  60.1 us (15%)
  other arithmetic  50.4 us (13%)
  matrix products  34.8 us (9%)
  starting transfers between devices  19.9 us (5%)
  between operations  14.1 us (4%)
    ppermute x4, waiting for transfers between devices, passed_along(): return lax.ppermute(value, axis, pairs)  77.1 us
    psum x1, blocking collectives, per_device(): glob_q, glob_k, glob_v = lax.psum((picked[0], picked[1], picked[2]), 'seq')  70.1 us
    all_gather x2, blocking collectives, merged_2(): gathered = jax.tree.map(lambda a: lax.all_gather(a, axis), part)  41.9 us
    all_gather x1, waiting for transfers between devices, per_device(): lax.all_gather(mlp_up, 'seq', axis=0, tiled=True)  27.4 us
    add x15, other arithmetic, join_partials(): numer_first * scale_first[:, :, None]  20.8 us
    ppermute x1, starting transfers between devices, with_halo(): lax.ppermute(tail, axis, [(i, (i + 1) % count) for i in range(count)])  15.3 us
    dot_general x1, matrix products, per_device(): jnp.dot(columns, lax.all_gather(mlp_down, 'seq', axis=0, tiled=True), pre...  12.4 us
    add x15, other arithmetic, join_partials(): total_first * scale_first + total_second * scale_second  11 us
  transfers between devices with their start and end apart: 9, of which 4 were waited for; matrix products, arithmetic and copies ran while one was open for 29% of the time, Pallas kernels for 0%

commit v1 on v0

--- a/solution.py
+++ b/solution.py
@@ -1,12 +1,51 @@
+import functools
 import jax
 import jax.numpy as jnp
 from jax import lax
 from jax.sharding import PartitionSpec as P
+from jax.lax import axis_index, axis_size, ppermute
 
 H = 12
 DH = 64
 BLK = 128
 GLOBALS = 64
+
+
+def tell_case(row_data, out_dim):
+    z_new, parts_out, current_arr = (axis_size("seq"), axis_index("seq"), row_data.shape[out_dim])
+    store = []
+    for h, i0 in enumerate(row_data.shape):
+        store.append(i0 * z_new if h == out_dim else i0)
+    tile_out = lax.dynamic_update_slice_in_dim(
+        jnp.zeros(store, row_data.dtype), row_data, parts_out * current_arr, axis=out_dim
+    )
+    r1 = wide_out = row_data
+    w = 1
+    while w < z_new // 2 + 1:
+        vals = []
+        h = 0
+        while h < z_new:
+            vals.append((h, (h + 1) % z_new))
+            h = h + 1
+        r1 = ppermute(r1, "seq", perm=vals)
+        tile_out = lax.dynamic_update_slice_in_dim(
+            tile_out, r1, (parts_out - w) % z_new * current_arr, axis=out_dim
+        )
+        if 2 * w < z_new:
+            column = []
+            h = 0
+            while h < z_new:
+                column.append((h, (h - 1) % z_new))
+                h += 1
+            wide_out = ppermute(wide_out, "seq", column)
+            tile_out = lax.dynamic_update_slice_in_dim(
+                tile_out, wide_out, (parts_out + w) % z_new * current_arr, axis=out_dim
+            )
+        w += 1
+    return tile_out
+
+
+connect_results = functools.partial(tell_case, out_dim=0)
 
 
 def with_halo(cells, sides, width):
@@ -140,11 +179,7 @@
         jnp.bfloat16
     )
     columns = attended
-    pre_act = jnp.dot(
-        columns,
-        lax.all_gather(mlp_up, "seq", axis=0, tiled=True),
-        preferred_element_type=jnp.float32,
-    )
+    pre_act = jnp.dot(columns, connect_results(mlp_up), preferred_element_type=jnp.float32)
     hidden = jax.nn.gelu(pre_act, approximate=True).astype(jnp.bfloat16)
     columns = hidden
     mlp_out = jnp.dot(

time: 400 us -> 454 us (1.14)
  the two profiles are of different devices: /device:TPU:0 before, /device:TPU:1 now
where the time goes in v1:
time: 454 us; the launch traced here: 451 us
  blocking collectives  125 us (28%)
  local copies, waits for them, and re-layouts  90.3 us (20%)
  starting transfers between devices  69.7 us (15%)
  waiting for transfers between devices  61.9 us (14%)
  other arithmetic  53.2 us (12%)
  matrix products  35.6 us (8%)
  between operations  14.6 us (3%)
    psum x1, blocking collectives, per_device(): glob_q, glob_k, glob_v = lax.psum((picked[0], picked[1], picked[2]), 'seq')  64.9 us
    all_gather x2, blocking collectives, merged_2(): gathered = jax.tree.map(lambda a: lax.all_gather(a, axis), part)  60.2 us
    ppermute x8, starting transfers between devices, tell_case(): r1 = ppermute(r1, 'seq', perm=vals)  57.8 us
    ppermute x8, waiting for transfers between devices, tell_case(): r1 = ppermute(r1, 'seq', perm=vals)  37.5 us
    add x15, other arithmetic, join_partials(): numer_first * scale_first[:, :, None]  20.7 us
    dynamic_update_slice x8, local copies, waits for them, and re-layouts, tell_case(): lax.dynamic_update_slice_in_dim(tile_out, r1, (parts_out - w) % z_new * c...  13.4 us
    ppermute x4, waiting for transfers between devices, passed_along(): return lax.ppermute(value, axis, pairs)  13.3 us
    dot_general x1, matrix products, per_device(): jnp.dot(columns, lax.all_gather(mlp_down, 'seq', axis=0, tiled=True), pre...  12.7 us
  transfers between devices with their start and end apart: 23, of which 7 were waited for; matrix products, arithmetic and copies ran while one was open for 33% of the time, Pallas kernels for 0%

profile of v1, /device:TPU:1, one launch (start us, length us, event | category | flops | bytes accessed | tf_op | source)
XLA Modules:
  0.0 450.8 jit_solution(5572688236832103760)
XLA Ops:
  13.1 1.9 copy.69
  16.9 64.9 %all-reduce.2 = (bf16[64,768]{1,0:T(8,128)(2,1)}, bf16[64,768]{1,0:T(8,128)(2,1)}, bf16[64,768]{1,0:T(8,128)(2,1)}) all-reduce(f32[64,768]{1,0:T(8,128)} %fusion.47, f32[64,768]{1,0:T(8,128)} %fusion.48, f32[64,768]{1,0:T(8,128)} %fusion.49), channel_id=1, replica_groups=mesh['group'=2,'seq'=16] {'seq'}, use_global_device_ids=true, to_apply=%region_7.8 | all-reduce | flops 147456 | bytes 884736 | tf_op jit(solution)/shard_map/psum | solution.py:147
  85.8 2.3 fusion.37
  89.9 3.7 collective-permute-start.7
  94.6 4.4 collective-permute-start.2
  108.1 40.5 %all-gather.4 = f32[16,12,64]{2,1,0:T(8,128)} all-gather(f32[1,12,64]{2,1,0:T(8,128)S(1)} %bitcast.103), channel_id=3, replica_groups=mesh['group'=2,'seq'=16] {'seq'}, dimensions={0}, use_global_device_ids=true | all-gather | bytes 52224 | tf_op jit(solution)/shard_map/all_gather | solution.py:74
  148.6 19.6 %all-gather.3 = f32[16,12,64]{2,1,0:T(8,128)} all-gather(f32[1,12,64]{2,1,0:T(8,128)S(1)} %bitcast.102), channel_id=2, replica_groups=mesh['group'=2,'seq'=16] {'seq'}, dimensions={0}, use_global_device_ids=true | all-gather | bytes 52224 | tf_op jit(solution)/shard_map/all_gather | solution.py:74
  180.3 4.8 %broadcast_in_dim.101 = bf16[1536,3072]{1,0:T(8,128)(2,1)} broadcast(bf16[]{:T(256)} %constant.174.clone.1), dimensions={} | broadcast | bytes 9437186 | tf_op jit(solution)/shard_map/broadcast_in_dim | solution.py:20
  188.5 2.4 pad_maximum_fusion.2
  190.9 2.6 copy.71
  193.5 3.5 reshape.91
  197.0 5.1 %fusion.65 = (bf16[2,2,128,12,64]{2,1,4,3,0:T(2,128)(2,1)S(1)}, bf16[2,2,128,12,64]{2,1,4,3,0:T(2,128)(2,1)S(1)}, bf16[2,2,128,12,64]{2,1,4,3,0:T(2,128)(2,1)S(1)}) fusion(bf16[2,4,128,12,64]{2,1,4,3,0:T(4,128)(2,1)} %reshape.91), kind=kLoop, calls=%fused_computation.114 | loop fusion | bytes 4718592 | tf_op jit(solution)/shard_map/slice | solution.py:153
  206.7 2.4 broadcast_select_fusion
  209.1 2.6 collective-permute-start.3
  213.6 1.9 constant_dynamic-update-slice_fusion.13
  215.6 2.3 copy.78
  217.8 2.7 reshape.95
  220.6 13.3 %collective-permute-done.8 = bf16[96,3072]{1,0:T(8,128)(2,1)} collective-permute-done((bf16[96,3072]{1,0:T(8,128)(2,1)}, bf16[96,3072]{1,0:T(8,128)(2,1)}, u32[]{:S(2)}, u32[]{:S(2)}) %collective-permute-start.8) | collective-permute-done | bytes 589856 | tf_op jit(solution)/shard_map/ppermute | solution.py:30
  233.9 2.6 collective-permute-start.10
  236.4 11.1 %collective-permute-done.9 = bf16[96,3072]{1,0:T(8,128)(2,1)} collective-permute-done((bf16[96,3072]{1,0:T(8,128)(2,1)}, bf16[96,3072]{1,0:T(8,128)(2,1)}, u32[]{:S(2)}, u32[]{:S(2)}) %collective-permute-start.9) | collective-permute-done | bytes 589856 | tf_op jit(solution)/shard_map/ppermute | solution.py:40
  247.5 1.9 constant_dynamic-update-slice_fusion.12
  249.4 8.2 %collective-permute-done.3 = bf16[2,256,768]{2,1,0:T(8,128)(2,1)} collective-permute-done((bf16[2,256,768]{2,1,0:T(8,128)(2,1)}, bf16[2,256,768]{2,1,0:T(8,128)(2,1)}, u32[]{:S(2)}, u32[]{:S(2)}) %collective-permute-start.3) | collective-permute-done | bytes 786464 | tf_op jit(solution)/shard_map/ppermute | solution.py:70
  257.6 2.4 broadcast_select_fusion.1
  260.0 1.9 constant_dynamic-update-slice_fusion.11
  264.4 10.2 %collective-permute-done.10 = bf16[96,3072]{1,0:T(8,128)(2,1)} collective-permute-done((bf16[96,3072]{1,0:T(8,128)(2,1)}, bf16[96,3072]{1,0:T(8,128)(2,1)}, u32[]{:S(2)}, u32[]{:S(2)}) %collective-permute-start.10) | collective-permute-done | bytes 589856 | tf_op jit(solution)/shard_map/ppermute | solution.py:30
  274.6 2.5 collective-permute-start.12
  277.7 1.9 constant_dynamic-update-slice_fusion.10
  279.6 1.9 constant_dynamic-update-slice_fusion.9
  281.5 5.1 %collective-permute-done.4 = bf16[2,256,768]{2,1,0:T(8,128)(2,1)} collective-permute-done((bf16[2,256,768]{2,1,0:T(8,128)(2,1)}, bf16[2,256,768]{2,1,0:T(8,128)(2,1)}, u32[]{:S(2)}, u32[]{:S(2)}) %collective-permute-start.4) | collective-permute-done | bytes 786464 | tf_op jit(solution)/shard_map/ppermute | solution.py:70
  286.6 2.3 broadcast_select_fusion.2
  289.0 34.6 %collective-permute-start.14 = (bf16[96,3072]{1,0:T(8,128)(2,1)}, bf16[96,3072]{1,0:T(8,128)(2,1)}, u32[]{:S(2)}, u32[]{:S(2)}) collective-permute-start(bf16[96,3072]{1,0:T(8,128)(2,1)} %collective-permute-done.12), channel_id=1, source_target_pairs={{0,1},{1,2},{2,3},{3,4},{4,5},{5,6},{6,7},{7,8},{8,9},{9,10},{10,1... | collective-permute-start | bytes 1769480 | tf_op jit(solution)/shard_map/ppermute | solution.py:30
  323.6 2.0 constant_dynamic-update-slice_fusion.8
  325.5 2.0 constant_dynamic-update-slice_fusion.7
  327.5 2.3 copy.76
  329.8 2.8 reshape.93
  334.3 1.9 constant_dynamic-update-slice_fusion.6
  338.1 2.3 copy.75
  340.4 2.7 reshape.92
  343.1 2.5 fusion.36
  349.2 7.1 %fusion.66 = (f32[2,12,128]{2,1,0:T(8,128)S(1)}, f32[2,12,128,576]{2,3,1,0:T(8,128)}) fusion(bf16[2,64,12,64]{1,3,2,0:T(8,128)(2,1)S(1)} %broadcast_in_dim.100, bf16[2,512,12,64]{1,3,2,0:T(8,128)(2,1)} %get-tuple-element.205, bf16[2,128,12,64]{1,0,3,2:T(2,128)(2,1)S(1)} %copy-done.8), kind=kOutput, calls=%fused_computation.115 | convolution fusion | flops 235340352 | bytes 9252864 | tf_op jit(solution)/shard_map/sub | solution.py:96
  356.4 4.3 fusion.30
  361.4 11.1 %collective-permute-start.18 = (bf16[96,3072]{1,0:T(8,128)(2,1)}, bf16[96,3072]{1,0:T(8,128)(2,1)S(1)}, u32[]{:S(2)}, u32[]{:S(2)}) collective-permute-start(bf16[96,3072]{1,0:T(8,128)(2,1)} %collective-permute-done.16), channel_id=1, source_target_pairs={{0,1},{1,2},{2,3},{3,4},{4,5},{5,6},{6,7},{7,8},{8,9},{9,10},{10,1... | collective-permute-start | bytes 1769480 | tf_op jit(solution)/shard_map/ppermute | solution.py:30
  372.5 2.0 constant_dynamic-update-slice_fusion.4
  376.3 8.9 %collective-permute-done.18 = bf16[96,3072]{1,0:T(8,128)(2,1)S(1)} collective-permute-done((bf16[96,3072]{1,0:T(8,128)(2,1)}, bf16[96,3072]{1,0:T(8,128)(2,1)S(1)}, u32[]{:S(2)}, u32[]{:S(2)}) %collective-permute-start.18) | collective-permute-done | bytes 589856 | tf_op jit(solution)/shard_map/ppermute | solution.py:30
  385.3 2.4 collective-permute-start.20
  389.4 5.1 %collective-permute-done.20 = bf16[96,3072]{1,0:T(8,128)(2,1)S(1)} collective-permute-done((bf16[96,3072]{1,0:T(8,128)(2,1)S(1)}, bf16[96,3072]{1,0:T(8,128)(2,1)S(1)}, u32[]{:S(2)}, u32[]{:S(2)}) %collective-permute-start.20) | collective-permute-done | bytes 589856 | tf_op jit(solution)/shard_map/ppermute | solution.py:30
  396.4 32.1 %while.19 = (s32[]{:T(128)}, f32[12,64]{1,0:T(8,128)S(1)}, f32[12,64]{1,0:T(8,128)S(1)}, f32[12,64,64]{2,1,0:T(8,128)S(1)}, f32[16,12,64]{2,1,0:T(8,128)}, /*ind...) while((s32[]{:T(128)}, f32[12,64]{1,0:T(8,128)S(1)}, ...), condition=%wide.region_5.6_spmd, body=%wide.region_4.5_spmd.sunk | while | flops 152069 | bytes 620695 | solution.py:79
  431.3 12.7 %convolution_convert_fusion = bf16[256,1536]{1,0:T(8,128)(2,1)} fusion(bf16[3072,1536]{1,0:T(8,128)(2,1)} %all-gather.8.cloned.1.call-done, bf16[256,1536]{1,0:T(8,128)(2,1)} %convolution_convert_fusion.1, bf16[1536,3072]{1,0:T(8,128)(2,1)} %constant_dynamic-update-slice_fusion), kind=kOutput, calls=%fused_computation.28 | convolution fusion | flops 4839309312 | bytes 20447232 | tf_op jit(solution)/shard_map/dot_general | solution.py:185
  (150 shorter events, 96.2 us)
Async XLA Ops:
  7.2 422.5 %copy-start = (bf16[768,1536]{1,0:T(8,128)(2,1)S(1)}, bf16[768,1536]{1,0:T(8,128)(2,1)}, u32[]{:S(2)}) copy-start(bf16[768,1536]{1,0:T(8,128)(2,1)} %param.15) | copy-start | bytes 7077892
  7.2 86.4 %copy-start.1 = (bf16[256,768]{1,0:T(8,128)(2,1)S(1)}, bf16[256,768]{1,0:T(8,128)(2,1)}, u32[]{:S(2)}) copy-start(bf16[256,768]{1,0:T(8,128)(2,1)} %param.11) | copy-start | bytes 1179652
  7.2 86.4 %copy-start.2 = (bf16[256,768]{1,0:T(8,128)(2,1)S(1)}, bf16[256,768]{1,0:T(8,128)(2,1)}, u32[]{:S(2)}) copy-start(bf16[256,768]{1,0:T(8,128)(2,1)} %param.12) | copy-start | bytes 1179652
  7.2 388.1 %all-gather.10.cloned.1.call-start = ((), (), s32[]{:S(2)}) async-start(), calls=%async_computation.1 | async-start | bytes 6684672 | tf_op jit(solution)/shard_map/all_gather | solution.py:74
  9.2 74.4 %copy-start.10 = (s32[64]{0:T(128)}, s32[64]{0:T(128)S(1)}, u32[]{:S(2)}) copy-start(s32[64]{0:T(128)S(1)} %broadcast_subtract_fusion) | copy-start | bytes 772
  84.9 0.9 copy-start.3
  88.2 343.1 %all-gather.8.cloned.1.call-start = ((), (), s32[]{:S(2)}) async-start(), calls=%async_computation | async-start | bytes 10027008 | tf_op jit(solution)/shard_map/all_gather | solution.py:187
  88.2 117.2 %collective-permute-start.6 = (bf16[96,3072]{1,0:T(8,128)(2,1)}, bf16[96,3072]{1,0:T(8,128)(2,1)}, u32[]{:S(2)}, u32[]{:S(2)}) collective-permute-start(bf16[96,3072]{1,0:T(8,128)(2,1)} %param.16), channel_id=1, source_target_pairs={{0,1},{1,2},{2,3},{3,4},{4,5},{5,6},{6,7},{7,8},{8,9},{9,10},{10,1... | collective-permute-start | bytes 1769480 | tf_op jit(solution)/shard_map/ppermute | solution.py:30
  89.9 116.8 %collective-permute-start.7 = (bf16[96,3072]{1,0:T(8,128)(2,1)}, bf16[96,3072]{1,0:T(8,128)(2,1)}, u32[]{:S(2)}, u32[]{:S(2)}) collective-permute-start(bf16[96,3072]{1,0:T(8,128)(2,1)} %param.16), channel_id=1, source_target_pairs={{0,15},{1,0},{2,1},{3,2},{4,3},{5,4},{6,5},{7,6},{8,7},{9,8},{10,9... | collective-permute-start | bytes 1769480 | tf_op jit(solution)/shard_map/ppermute | solution.py:40
  94.6 112.2 %collective-permute-start.2 = (bf16[2,256,768]{2,1,0:T(8,128)(2,1)}, bf16[2,256,768]{2,1,0:T(8,128)(2,1)}, u32[]{:S(2)}, u32[]{:S(2)}) collective-permute-start(bf16[2,256,768]{2,1,0:T(8,128)(2,1)} %pad_maximum_fusion.9), channel_id=1, source_target_pairs={{0,15},{1,0},{2,1},{3,2},{4,3},{5,4},{6,5},{7,6},{8,7},{9,8},{10,9... | collective-permute-start | bytes 2359304 | tf_op jit(solution)/shard_map/ppermute | solution.py:70
  99.9 88.6 %collective-permute-start = (bf16[2,128,768]{2,1,0:T(8,128)(2,1)}, bf16[2,128,768]{2,1,0:T(8,128)(2,1)}, u32[]{:S(2)}, u32[]{:S(2)}) collective-permute-start(bf16[2,128,768]{2,1,0:T(8,128)(2,1)} %get-tuple-element.209), channel_id=1, source_target_pairs={{0,1},{1,2},{2,3},{3,4},{4,5},{5,6},{6,7},{7,8},{8,9},{9,10},{10,1... | collective-permute-start | bytes 1179656 | tf_op jit(solution)/shard_map/ppermute | solution.py:58
  99.9 88.6 %collective-permute-start.1 = (bf16[2,128,768]{2,1,0:T(8,128)(2,1)}, bf16[2,128,768]{2,1,0:T(8,128)(2,1)}, u32[]{:S(2)}, u32[]{:S(2)}) collective-permute-start(bf16[2,128,768]{2,1,0:T(8,128)(2,1)} %get-tuple-element.210), channel_id=1, source_target_pairs={{1,0},{2,1},{3,2},{4,3},{5,4},{6,5},{7,6},{8,7},{9,8},{10,9},{11,1... | collective-permute-start | bytes 1179656 | tf_op jit(solution)/shard_map/ppermute | solution.py:60
  169.5 0.6 copy-start.14
  169.5 2.0 copy-start.12
  169.5 2.0 copy-start.13
  180.3 4.8 %copy-start.7 = (bf16[96,3072]{1,0:T(8,128)(2,1)S(1)}, bf16[96,3072]{1,0:T(8,128)(2,1)}, u32[]{:S(2)}) copy-start(bf16[96,3072]{1,0:T(8,128)(2,1)} %param.16) | copy-start | bytes 1769476
  197.0 9.7 %copy-start.9 = (pred[768]{0:T(1024)(128)(4,1)S(1)}, pred[768]{0:T(1024)(128)(4,1)}, u32[]{:S(2)}) copy-start(pred[768]{0:T(1024)(128)(4,1)} %broadcast_in_dim.92) | copy-start | bytes 2308
  205.4 28.4 %collective-permute-start.8 = (bf16[96,3072]{1,0:T(8,128)(2,1)}, bf16[96,3072]{1,0:T(8,128)(2,1)}, u32[]{:S(2)}, u32[]{:S(2)}) collective-permute-start(bf16[96,3072]{1,0:T(8,128)(2,1)} %collective-permute-done.6), channel_id=1, source_target_pairs={{0,1},{1,2},{2,3},{3,4},{4,5},{5,6},{6,7},{7,8},{8,9},{9,10},{10,1... | collective-permute-start | bytes 1769480 | tf_op jit(solution)/shard_map/ppermute | solution.py:30
  206.7 40.8 %collective-permute-start.9 = (bf16[96,3072]{1,0:T(8,128)(2,1)}, bf16[96,3072]{1,0:T(8,128)(2,1)}, u32[]{:S(2)}, u32[]{:S(2)}) collective-permute-start(bf16[96,3072]{1,0:T(8,128)(2,1)} %collective-permute-done.7), channel_id=1, source_target_pairs={{0,15},{1,0},{2,1},{3,2},{4,3},{5,4},{6,5},{7,6},{8,7},{9,8},{10,9... | collective-permute-start | bytes 1769480 | tf_op jit(solution)/shard_map/ppermute | solution.py:40
  209.1 48.5 %collective-permute-start.3 = (bf16[2,256,768]{2,1,0:T(8,128)(2,1)}, bf16[2,256,768]{2,1,0:T(8,128)(2,1)}, u32[]{:S(2)}, u32[]{:S(2)}) collective-permute-start(bf16[2,256,768]{2,1,0:T(8,128)(2,1)} %broadcast_select_fusion), channel_id=1, source_target_pairs={{0,14},{1,15},{2,0},{3,1},{4,2},{5,3},{6,4},{7,5},{8,6},{9,7},{10,... | collective-permute-start | bytes 2359304 | tf_op jit(solution)/shard_map/ppermute | solution.py:70
  233.9 40.7 %collective-permute-start.10 = (bf16[96,3072]{1,0:T(8,128)(2,1)}, bf16[96,3072]{1,0:T(8,128)(2,1)}, u32[]{:S(2)}, u32[]{:S(2)}) collective-permute-start(bf16[96,3072]{1,0:T(8,128)(2,1)} %collective-permute-done.8), channel_id=1, source_target_pairs={{0,1},{1,2},{2,3},{3,4},{4,5},{5,6},{6,7},{7,8},{8,9},{9,10},{10,1... | collective-permute-start | bytes 1769480 | tf_op jit(solution)/shard_map/ppermute | solution.py:30
  247.5 29.6 %collective-permute-start.11 = (bf16[96,3072]{1,0:T(8,128)(2,1)}, bf16[96,3072]{1,0:T(8,128)(2,1)}, u32[]{:S(2)}, u32[]{:S(2)}) collective-permute-start(bf16[96,3072]{1,0:T(8,128)(2,1)} %collective-permute-done.9), channel_id=1, source_target_pairs={{0,15},{1,0},{2,1},{3,2},{4,3},{5,4},{6,5},{7,6},{8,7},{9,8},{10,9... | collective-permute-start | bytes 1769480 | tf_op jit(solution)/shard_map/ppermute | solution.py:40
  260.0 26.6 %collective-permute-start.4 = (bf16[2,256,768]{2,1,0:T(8,128)(2,1)}, bf16[2,256,768]{2,1,0:T(8,128)(2,1)}, u32[]{:S(2)}, u32[]{:S(2)}) collective-permute-start(bf16[2,256,768]{2,1,0:T(8,128)(2,1)} %broadcast_select_fusion.1), channel_id=1, source_target_pairs={{0,12},{1,13},{2,14},{3,15},{4,0},{5,1},{6,2},{7,3},{8,4},{9,5},{1... | collective-permute-start | bytes 2359304 | tf_op jit(solution)/shard_map/ppermute | solution.py:70
  274.6 14.4 %collective-permute-start.12 = (bf16[96,3072]{1,0:T(8,128)(2,1)}, bf16[96,3072]{1,0:T(8,128)(2,1)}, u32[]{:S(2)}, u32[]{:S(2)}) collective-permute-start(bf16[96,3072]{1,0:T(8,128)(2,1)} %collective-permute-done.10), channel_id=1, source_target_pairs={{0,1},{1,2},{2,3},{3,4},{4,5},{5,6},{6,7},{7,8},{8,9},{9,10},{10,1... | collective-permute-start | bytes 1769480 | tf_op jit(solution)/shard_map/ppermute | solution.py:30
  277.1 46.5 %collective-permute-start.13 = (bf16[96,3072]{1,0:T(8,128)(2,1)}, bf16[96,3072]{1,0:T(8,128)(2,1)}, u32[]{:S(2)}, u32[]{:S(2)}) collective-permute-start(bf16[96,3072]{1,0:T(8,128)(2,1)} %collective-permute-done.11), channel_id=1, source_target_pairs={{0,15},{1,0},{2,1},{3,2},{4,3},{5,4},{6,5},{7,6},{8,7},{9,8},{10,9... | collective-permute-start | bytes 1769480 | tf_op jit(solution)/shard_map/ppermute | solution.py:40
  289.0 49.2 %collective-permute-start.5 = (bf16[2,256,768]{2,1,0:T(8,128)(2,1)}, bf16[2,256,768]{2,1,0:T(8,128)(2,1)}, u32[]{:S(2)}, u32[]{:S(2)}) collective-permute-start(bf16[2,256,768]{2,1,0:T(8,128)(2,1)} %broadcast_select_fusion.2), channel_id=1, source_target_pairs={{0,8},{1,9},{2,10},{3,11},{4,12},{5,13},{6,14},{7,15},{8,0},{9,1},... | collective-permute-start | bytes 2359304 | tf_op jit(solution)/shard_map/ppermute | solution.py:70
  289.0 43.6 %collective-permute-start.14 = (bf16[96,3072]{1,0:T(8,128)(2,1)}, bf16[96,3072]{1,0:T(8,128)(2,1)}, u32[]{:S(2)}, u32[]{:S(2)}) collective-permute-start(bf16[96,3072]{1,0:T(8,128)(2,1)} %collective-permute-done.12), channel_id=1, source_target_pairs={{0,1},{1,2},{2,3},{3,4},{4,5},{5,6},{6,7},{7,8},{8,9},{9,10},{10,1... | collective-permute-start | bytes 1769480 | tf_op jit(solution)/shard_map/ppermute | solution.py:30
  323.6 10.7 %collective-permute-start.15 = (bf16[96,3072]{1,0:T(8,128)(2,1)}, bf16[96,3072]{1,0:T(8,128)(2,1)}, u32[]{:S(2)}, u32[]{:S(2)}) collective-permute-start(bf16[96,3072]{1,0:T(8,128)(2,1)} %collective-permute-done.13), channel_id=1, source_target_pairs={{0,15},{1,0},{2,1},{3,2},{4,3},{5,4},{6,5},{7,6},{8,7},{9,8},{10,9... | collective-permute-start | bytes 1769480 | tf_op jit(solution)/shard_map/ppermute | solution.py:40
  329.8 15.8 %copy-start.4 = (bf16[2,2,128,12,64]{2,4,3,1,0:T(8,128)(2,1)S(1)}, bf16[2,2,128,12,64]{2,4,3,1,0:T(8,128)(2,1)}, u32[]{:S(2)}) copy-start(bf16[2,2,128,12,64]{2,4,3,1,0:T(8,128)(2,1)} %copy.95) | copy-start | bytes 2359300
  332.6 28.8 %collective-permute-start.16 = (bf16[96,3072]{1,0:T(8,128)(2,1)}, bf16[96,3072]{1,0:T(8,128)(2,1)}, u32[]{:S(2)}, u32[]{:S(2)}) collective-permute-start(bf16[96,3072]{1,0:T(8,128)(2,1)} %collective-permute-done.14), channel_id=1, source_target_pairs={{0,1},{1,2},{2,3},{3,4},{4,5},{5,6},{6,7},{7,8},{8,9},{9,10},{10,1... | collective-permute-start | bytes 1769480 | tf_op jit(solution)/shard_map/ppermute | solution.py:30
  334.3 38.2 %collective-permute-start.17 = (bf16[96,3072]{1,0:T(8,128)(2,1)}, bf16[96,3072]{1,0:T(8,128)(2,1)}, u32[]{:S(2)}, u32[]{:S(2)}) collective-permute-start(bf16[96,3072]{1,0:T(8,128)(2,1)} %collective-permute-done.15), channel_id=1, source_target_pairs={{0,15},{1,0},{2,1},{3,2},{4,3},{5,4},{6,5},{7,6},{8,7},{9,8},{10,9... | collective-permute-start | bytes 1769480 | tf_op jit(solution)/shard_map/ppermute | solution.py:40
  345.6 3.5 copy-start.6
  345.6 3.6 copy-start.8
  349.2 7.1 %copy-start.5 = (bf16[64,768]{0,1:T(8,128)(2,1)S(1)}, bf16[64,768]{0,1:T(8,128)(2,1)}, u32[]{:S(2)}) copy-start(bf16[64,768]{0,1:T(8,128)(2,1)} %copy.93) | copy-start | bytes 294916
  361.4 23.9 %collective-permute-start.18 = (bf16[96,3072]{1,0:T(8,128)(2,1)}, bf16[96,3072]{1,0:T(8,128)(2,1)S(1)}, u32[]{:S(2)}, u32[]{:S(2)}) collective-permute-start(bf16[96,3072]{1,0:T(8,128)(2,1)} %collective-permute-done.16), channel_id=1, source_target_pairs={{0,1},{1,2},{2,3},{3,4},{4,5},{5,6},{6,7},{7,8},{8,9},{9,10},{10,1... | collective-permute-start | bytes 1769480 | tf_op jit(solution)/shard_map/ppermute | solution.py:30
  372.5 16.1 %collective-permute-start.19 = (bf16[96,3072]{1,0:T(8,128)(2,1)}, bf16[96,3072]{1,0:T(8,128)(2,1)S(1)}, u32[]{:S(2)}, u32[]{:S(2)}) collective-permute-start(bf16[96,3072]{1,0:T(8,128)(2,1)} %collective-permute-done.17), channel_id=1, source_target_pairs={{0,15},{1,0},{2,1},{3,2},{4,3},{5,4},{6,5},{7,6},{8,7},{9,8},{10,9... | collective-permute-start | bytes 1769480 | tf_op jit(solution)/shard_map/ppermute | solution.py:40
  385.3 9.2 %collective-permute-start.20 = (bf16[96,3072]{1,0:T(8,128)(2,1)S(1)}, bf16[96,3072]{1,0:T(8,128)(2,1)S(1)}, u32[]{:S(2)}, u32[]{:S(2)}) collective-permute-start(bf16[96,3072]{1,0:T(8,128)(2,1)S(1)} %collective-permute-done.18), channel_id=1, source_target_pairs={{0,1},{1,2},{2,3},{3,4},{4,5},{5,6},{6,7},{7,8},{8,9},{9,10},{10,1... | collective-permute-start | bytes 1769480 | tf_op jit(solution)/shard_map/ppermute | solution.py:30
  388.5 40.5 %copy-start.11 = (s32[64]{0:T(128)S(1)}, s32[64]{0:T(128)}, u32[]{:S(2)}) copy-start(s32[64]{0:T(128)} %copy-done.10) | copy-start | bytes 772
  388.5 40.5 %copy-start.15 = (pred[256]{0:T(512)(128)(4,1)S(1)}, pred[256]{0:T(512)(128)(4,1)}, u32[]{:S(2)}) copy-start(pred[256]{0:T(512)(128)(4,1)} %broadcast_compare_fusion) | copy-start | bytes 772
Sparse Core Ops, SparseCore 0:
  88.3 81.6 all-gather.9
  172.3 116.9 all-gather.7
